TPU v7x, 32 devices: a whole 2x2x4 slice. The times are simulated.
32 devices in a mesh: dp: 8 (over y, x, core), tensor: 4 (over z).
Axes of the slice: x: 2, y: 2, z: 4, core: 2. Of those that a mesh axis runs over, the one named last changes fastest.
Arguments:
- inputs: bfloat16 [64, 256, 1152], P('dp'), may hold values from -6 to 6
- cotangent: bfloat16 [64, 256, 1152], P('dp'), may hold values from -6 to 6
- counts: int32 [8], P('dp'), may hold values from 1 to 8, as said below
- time_ids: int32 [64], P('dp'), may hold values from 0 to 999
- class_ids: int32 [64], P('dp'), may hold values from 0 to 1000
- time_table: bfloat16 [1000, 1152], replicated, may hold values from -4 to 4
- class_table: bfloat16 [1001, 1152], replicated, may hold values from -4 to 4
- ada_weight: bfloat16 [1152, 6, 1152], P(None, None, 'tensor'), may hold values from -0.1875 to 0.1875
- ada_bias: bfloat16 [6, 1152], P(None, 'tensor'), may hold values from -1.75 to 1.75
- qkv_weight: bfloat16 [1152, 3, 1152], P(None, None, 'tensor'), may hold values from -0.1875 to 0.1875
- qv_bias: bfloat16 [2, 1152], P(None, 'tensor'), may hold values from -1.75 to 1.75
- proj_weight: bfloat16 [1152, 1152], P('tensor'), may hold values from -1.5 to 1.5
- proj_bias: bfloat16 [1152], replicated, may hold values from -1.75 to 1.75
- up_weight: bfloat16 [1152, 4608], P(None, 'tensor'), may hold values from -0.1875 to 0.1875
- up_bias: bfloat16 [4608], P('tensor'), may hold values from -1.75 to 1.75
- down_weight: bfloat16 [4608, 1152], P('tensor'), may hold values from -0.09375 to 0.09375
- down_bias: bfloat16 [1152], replicated, may hold values from -1.75 to 1.75
Outputs:
- outputs: bfloat16 [64, 256, 1152], P('dp')
- grad_inputs: bfloat16 [64, 256, 1152], P('dp')
- grad_time_table: float32 [1000, 1152], replicated
- grad_class_table: float32 [1001, 1152], replicated
- grad_ada_weight: float32 [1152, 6, 1152], P(None, None, 'tensor')
- grad_ada_bias: float32 [6, 1152], P(None, 'tensor')
- grad_qkv_weight: float32 [1152, 3, 1152], P(None, None, 'tensor')
- grad_qv_bias: float32 [2, 1152], P(None, 'tensor')
- grad_proj_weight: float32 [1152, 1152], P('tensor')
- grad_proj_bias: float32 [1152], replicated
- grad_up_weight: float32 [1152, 4608], P(None, 'tensor')
- grad_up_bias: float32 [4608], P('tensor')
- grad_down_weight: float32 [4608, 1152], P('tensor')
- grad_down_bias: float32 [1152], replicated
Inputs may be any that keep to these rules, and one draw needn't show every extreme that they name: Each index of dp holds 8 image slots whose first counts live; at least one index has all 8 live.
All inputs are finite; a program needn't handle non-finite values.
Results may differ from a plain program's by a relative error of at most 0.014.
The roundings to bfloat16 on the way count: a program that leaves them out, or rounds other values in their place, can miss the bound.
Values sent between devices are 32-bit elements; how exact they have to be, the bound alone decides.
No kernel may reach another device: no remote copies, remote signals or barrier semaphores. Data moves between devices by JAX's collectives and lax.ppermute only.
A program may use at most 256 MiB of HBM per device.

v0:
```python
import jax
import jax.numpy as jnp
from jax import lax
from jax.sharding import PartitionSpec as P

HEAD_DIM = 72
EPSILON = 1e-06
GELU_ROOT = 0.7978845608028654
GELU_CUBIC = 0.044715


def norm_parts(values):
    average = jnp.mean(values, axis=-1, keepdims=True)
    centred = values - average
    spread = jnp.mean(centred * centred, axis=-1, keepdims=True)
    inverse = lax.rsqrt(spread + EPSILON)
    return (centred * inverse, inverse)


def norm_back(upstream, normed, inverse):
    first_mean = jnp.mean(upstream, axis=-1, keepdims=True)
    second_mean = jnp.mean(upstream * normed, axis=-1, keepdims=True)
    return inverse * (upstream - first_mean - normed * second_mean)


def gelu_parts(values):
    argument = GELU_ROOT * (values + GELU_CUBIC * values * values * values)
    tangent = jnp.tanh(argument)
    result = 0.5 * values * (1.0 + tangent)
    derivative = 0.5 * (1.0 + tangent) + 0.5 * values * (1.0 - tangent * tangent) * GELU_ROOT * (
        1.0 + 3.0 * GELU_CUBIC * values * values
    )
    return (result, derivative)


def local(
    inputs,
    cotangent,
    counts,
    time_ids,
    class_ids,
    time_table,
    class_table,
    ada_weight,
    ada_bias,
    qkv_weight,
    qv_bias,
    proj_weight,
    proj_bias,
    up_weight,
    up_bias,
    down_weight,
    down_bias,
):
    wide = jnp.float32
    narrow = jnp.bfloat16
    images, length, width = inputs.shape
    local_width = qkv_weight.shape[2]
    heads_here = local_width // HEAD_DIM
    scaling = HEAD_DIM ** (-0.5)
    live = (jnp.arange(images, dtype=jnp.int32) < counts[0]).astype(wide)
    time_levels = jnp.arange(time_table.shape[0], dtype=jnp.int32)
    class_levels = jnp.arange(class_table.shape[0], dtype=jnp.int32)
    time_pick = (time_ids[:, None] == time_levels[None, :]).astype(narrow)
    class_pick = (class_ids[:, None] == class_levels[None, :]).astype(narrow)
    condition = jnp.dot(time_pick, time_table, preferred_element_type=wide) + jnp.dot(
        class_pick, class_table, preferred_element_type=wide
    )
    silu_cond = jax.nn.silu(condition).astype(narrow)
    mod_local = jnp.einsum(
        "gd,dke->gke", silu_cond, ada_weight, preferred_element_type=wide
    ) + ada_bias.astype(wide)
    modulation = lax.all_gather(mod_local, "tensor", axis=2, tiled=True)
    shift_attn = modulation[:, 0, None, :]
    scale_attn = modulation[:, 1, None, :]
    gate_attn = modulation[:, 2, None, :]
    shift_mlp = modulation[:, 3, None, :]
    scale_mlp = modulation[:, 4, None, :]
    gate_mlp = modulation[:, 5, None, :]
    input_wide = inputs.astype(wide)
    normed_attn, inverse_attn = norm_parts(input_wide)
    hidden_attn = (normed_attn * (1.0 + scale_attn) + shift_attn).astype(narrow)
    projected = jnp.einsum("gsd,dke->gske", hidden_attn, qkv_weight, preferred_element_type=wide)
    bias_wide = qv_bias.astype(wide)
    shape_heads = (images, length, heads_here, HEAD_DIM)
    query_heads = (projected[:, :, 0] + bias_wide[0]).astype(narrow).reshape(shape_heads)
    key_heads = projected[:, :, 1].astype(narrow).reshape(shape_heads)
    value_heads = (projected[:, :, 2] + bias_wide[1]).astype(narrow).reshape(shape_heads)
    scores = (
        jnp.einsum("gqhe,gkhe->ghqk", query_heads, key_heads, preferred_element_type=wide) * scaling
    )
    highest = jnp.max(scores, axis=-1, keepdims=True)
    exponent = jnp.exp(scores - highest)
    denominator = jnp.sum(exponent, axis=-1, keepdims=True)
    soft_probs = (exponent / denominator).astype(narrow)
    log_total = highest + jnp.log(denominator)
    heads_out = jnp.einsum("ghqk,gkhe->gqhe", soft_probs, value_heads, preferred_element_type=wide)
    heads_out = heads_out.reshape(images, length, local_width).astype(narrow)
    attn_part = jnp.einsum("gse,ed->gsd", heads_out, proj_weight, preferred_element_type=wide)
    attention = lax.psum(attn_part, "tensor") + proj_bias.astype(wide)
    middle = input_wide + gate_attn * attention
    normed_mlp, inverse_mlp = norm_parts(middle)
    hidden_mlp = (normed_mlp * (1.0 + scale_mlp) + shift_mlp).astype(narrow)
    pre_act = jnp.einsum(
        "gsd,df->gsf", hidden_mlp, up_weight, preferred_element_type=wide
    ) + up_bias.astype(wide)
    gelu_value, gelu_slope = gelu_parts(pre_act)
    activated = gelu_value.astype(narrow)
    mlp_part = jnp.einsum("gsf,fd->gsd", activated, down_weight, preferred_element_type=wide)
    branch = lax.psum(mlp_part, "tensor") + down_bias.astype(wide)
    outputs = ((middle + gate_mlp * branch) * live[:, None, None]).astype(narrow)
    grad_out = cotangent.astype(wide) * live[:, None, None]
    d_gate_mlp = jnp.sum(grad_out * branch, axis=1)
    d_branch = (gate_mlp * grad_out).astype(narrow)
    grad_down_bias = jnp.sum(d_branch, axis=(0, 1), dtype=wide)
    grad_down_weight = jnp.einsum("gsf,gsd->fd", activated, d_branch, preferred_element_type=wide)
    d_activated = jnp.einsum("gsd,fd->gsf", d_branch, down_weight, preferred_element_type=wide)
    d_pre = (d_activated * gelu_slope).astype(narrow)
    grad_up_bias = jnp.sum(d_pre, axis=(0, 1), dtype=wide)
    grad_up_weight = jnp.einsum("gsd,gsf->df", hidden_mlp, d_pre, preferred_element_type=wide)
    grad_down_weight, grad_down_bias, grad_up_weight, grad_up_bias = lax.psum(
        (grad_down_weight, grad_down_bias, grad_up_weight, grad_up_bias), "dp"
    )
    d_mlp_part = jnp.einsum("gsf,df->gsd", d_pre, up_weight, preferred_element_type=wide)
    d_hidden_mlp = lax.psum(d_mlp_part, "tensor")
    d_shift_mlp = jnp.sum(d_hidden_mlp, axis=1)
    d_scale_mlp = jnp.sum(d_hidden_mlp * normed_mlp, axis=1)
    d_middle = grad_out + norm_back(d_hidden_mlp * (1.0 + scale_mlp), normed_mlp, inverse_mlp)
    d_gate_attn = jnp.sum(d_middle * attention, axis=1)
    d_attention = (gate_attn * d_middle).astype(narrow)
    grad_proj_bias = jnp.sum(d_attention, axis=(0, 1), dtype=wide)
    grad_proj_weight = jnp.einsum(
        "gse,gsd->ed", heads_out, d_attention, preferred_element_type=wide
    )
    d_heads = jnp.einsum("gsd,ed->gse", d_attention, proj_weight, preferred_element_type=wide)
    d_heads = d_heads.astype(narrow).reshape(shape_heads)
    scores_again = (
        jnp.einsum("gqhe,gkhe->ghqk", query_heads, key_heads, preferred_element_type=wide) * scaling
    )
    probs_again = jnp.exp(scores_again - log_total)
    d_value = jnp.einsum(
        "ghqk,gqhe->gkhe", probs_again.astype(narrow), d_heads, preferred_element_type=wide
    )
    d_value = d_value.astype(narrow)
    d_probs = jnp.einsum("gqhe,gkhe->ghqk", d_heads, value_heads, preferred_element_type=wide)
    row_inner = jnp.sum(probs_again * d_probs, axis=-1, keepdims=True)
    d_scores = (probs_again * (d_probs - row_inner)).astype(narrow)
    d_query = (
        jnp.einsum("ghqk,gkhe->gqhe", d_scores, key_heads, preferred_element_type=wide) * scaling
    ).astype(narrow)
    d_key = (
        jnp.einsum("ghqk,gqhe->gkhe", d_scores, query_heads, preferred_element_type=wide) * scaling
    ).astype(narrow)
    d_projected = jnp.stack([d_query, d_key, d_value], axis=2).reshape(
        images, length, 3, local_width
    )
    grad_qv_bias = jnp.stack(
        [
            jnp.sum(d_query, axis=(0, 1), dtype=wide).reshape(local_width),
            jnp.sum(d_value, axis=(0, 1), dtype=wide).reshape(local_width),
        ],
        axis=0,
    )
    grad_qkv_weight = jnp.einsum(
        "gsd,gske->dke", hidden_attn, d_projected, preferred_element_type=wide
    )
    d_attn_part = jnp.einsum("gske,dke->gsd", d_projected, qkv_weight, preferred_element_type=wide)
    d_hidden_attn = lax.psum(d_attn_part, "tensor")
    d_shift_attn = jnp.sum(d_hidden_attn, axis=1)
    d_scale_attn = jnp.sum(d_hidden_attn * normed_attn, axis=1)
    grad_inputs = (
        d_middle + norm_back(d_hidden_attn * (1.0 + scale_attn), normed_attn, inverse_attn)
    ).astype(narrow)
    d_modulation = jnp.stack(
        [d_shift_attn, d_scale_attn, d_gate_attn, d_shift_mlp, d_scale_mlp, d_gate_mlp], axis=1
    ).astype(narrow)
    start_column = lax.axis_index("tensor") * local_width
    d_mod_local = lax.dynamic_slice_in_dim(d_modulation, start_column, local_width, 2)
    grad_ada_weight = jnp.einsum("gd,gke->dke", silu_cond, d_mod_local, preferred_element_type=wide)
    grad_ada_bias = jnp.sum(d_mod_local, axis=0, dtype=wide)
    (
        grad_qkv_weight,
        grad_qv_bias,
        grad_proj_weight,
        grad_proj_bias,
        grad_ada_weight,
        grad_ada_bias,
    ) = lax.psum(
        (
            grad_qkv_weight,
            grad_qv_bias,
            grad_proj_weight,
            grad_proj_bias,
            grad_ada_weight,
            grad_ada_bias,
        ),
        "dp",
    )
    sigmoid_cond = jax.nn.sigmoid(condition)
    d_condition = jnp.einsum("gke,dke->gd", d_mod_local, ada_weight, preferred_element_type=wide)
    d_condition = d_condition * sigmoid_cond * (1.0 + condition * (1.0 - sigmoid_cond))
    exact = lax.Precision.HIGHEST
    grad_time_table = jnp.dot(time_pick.astype(wide).T, d_condition, precision=exact)
    grad_class_table = jnp.dot(class_pick.astype(wide).T, d_condition, precision=exact)
    grad_time_table, grad_class_table = lax.psum(
        (grad_time_table, grad_class_table), ("dp", "tensor")
    )
    return (
        outputs,
        grad_inputs,
        grad_time_table,
        grad_class_table,
        grad_ada_weight,
        grad_ada_bias,
        grad_qkv_weight,
        grad_qv_bias,
        grad_proj_weight,
        grad_proj_bias,
        grad_up_weight,
        grad_up_bias,
        grad_down_weight,
        grad_down_bias,
    )


def solution(mesh):
    in_specs = (
        P("dp", None, None),
        P("dp", None, None),
        P("dp"),
        P("dp"),
        P("dp"),
        P(),
        P(),
        P(None, None, "tensor"),
        P(None, "tensor"),
        P(None, None, "tensor"),
        P(None, "tensor"),
        P("tensor", None),
        P(),
        P(None, "tensor"),
        P("tensor"),
        P("tensor", None),
        P(),
    )
    out_specs = (
        P("dp", None, None),
        P("dp", None, None),
        P(),
        P(),
        P(None, None, "tensor"),
        P(None, "tensor"),
        P(None, None, "tensor"),
        P(None, "tensor"),
        P("tensor", None),
        P(),
        P(None, "tensor"),
        P("tensor"),
        P("tensor", None),
        P(),
    )
    return jax.shard_map(local, mesh=mesh, in_specs=in_specs, out_specs=out_specs, check_vma=False)
```

profile of v0, /device:TPU:0, one launch (start us, length us, event | category | flops | bytes accessed | tf_op | source)
XLA Modules:
  0.0 2098.7 jit_solution(2705256795855632784)
XLA Ops:
  7.3 3.2 convert_reduce_fusion
  10.5 4.5 fusion.14
  16.7 1.3 convolution_add_fusion.1
  18.0 1.5 copy.58
  19.4 91.1 %all_gather.3 = f32[8,6,1152]{1,0,2:T(8,128)} all-gather(f32[8,6,288]{1,0,2:T(8,128)} %copy.58), channel_id=1, replica_groups=mesh['dp'=8,'tensor'=4] {'tensor'}, dimensions={2}, use_global_device_ids=true | all-gather | bytes 276480 | tf_op jit(solution)/shard_map/all_gather | solution.py:73
  110.5 22.1 %fusion.73 = (f32[8,1,1152]{1,0,2:T(8,128)}, f32[8,1,1152]{1,0,2:T(8,128)}, f32[8,1,1152]{1,0,2:T(8,128)}, f32[8,1,1152]{1,0,2:T(8,128)}, f32[8,1,1152]{1,0,2:T(8,128)}, /*index=5*/f32[8,1,1152]{1,0,2:T(8,128)}) fusion(f32[8,6,1152]{1,0,2:T(8,128)} %all_gather.3), kind=kLoop, calls=%fused_computation.140 | loop fusion | bytes 442368 | tf_op jit(solution)/shard_map/slice | solution.py:79
  132.6 3.3 copy.86
  135.9 3.3 copy.85
  139.3 7.8 fusion.40
  147.2 1.1 slice.59
  148.3 2.7 fusion.72
  151.2 3.5 multiply_reduce_fusion.8
  154.7 1.6 fusion.22
  156.4 2.2 fusion.42
  158.6 1.0 copy-done.17
  159.6 5.4 fusion.49
  165.7 3.3 copy.87
  169.1 3.6 copy.88
  172.7 3.3 copy.84
  176.1 3.9 copy.89
  180.0 310.3 %all-reduce.10.cloned.1.call-done = f32[8,256,1152]{2,1,0:T(8,128)} async-done(((f32[8,256,1152]{2,1,0:T(8,128)}), f32[8,256,1152]{2,1,0:T(8,128)}) %all-reduce.10.cloned.1.call-update) | async-done | bytes 9437200 | tf_op jit(solution)/shard_map/psum | solution.py:100
  490.3 10.4 fusion.71
  500.7 4.9 multiply_reduce_fusion.4
  505.7 1.4 copy-done.2
  507.1 9.6 fusion.35
  516.7 12.8 convert_reduce_fusion.2
  529.5 2.3 copy-done.59
  531.8 9.6 fusion.33
  542.2 13.1 fusion.31
  555.3 309.9 %all-reduce.12.cloned.1.call-done = f32[8,256,1152]{2,1,0:T(8,128)} async-done(((f32[8,256,1152]{2,1,0:T(8,128)}), f32[8,256,1152]{2,1,0:T(8,128)}) %all-reduce.12.cloned.1.call-update) | async-done | bytes 9437200 | tf_op jit(solution)/shard_map/psum | solution.py:125
  865.2 8.5 multiply_reduce_fusion.1
  874.4 11.4 convert_reduce_fusion.3
  885.8 1.7 convolution_convert_fusion
  888.2 1.5 slice-done
  889.7 1.3 slice-done.1
  891.0 1.8 convert_reduce_fusion.4
  892.8 2.6 multiply_reduce_fusion.5
  895.4 2.5 multiply_convert_fusion.4
  897.9 1.4 multiply_convert_fusion.5
  899.4 1.0 convert_reduce_fusion.5
  900.4 7.9 convolution_bitcast_fusion.2
  909.1 16.6 convolution_bitcast_fusion
  925.7 611.2 %all-reduce.18.cloned.1.call-done = (f32[8,256,1152]{2,1,0:T(8,128)}, f32[8,256,1152]{2,1,0:T(8,128)}) async-done(((f32[8,256,1152]{2,1,0:T(8,128)}, f32[8,256,1152]{2,1,0:T(8,128)}), (f32[8,256,1152]{2,1,0:T(8,128)}, f32[8,256,1152]{2,1,0:T(8,128)})) %all-reduce.18.cloned.1.call-update) | async-done | bytes 18874384 | tf_op jit(solution)/shard_map/psum | solution.py:110
  1537.0 8.8 fusion.13
  1545.9 13.2 convert_reduce_fusion.1
  1559.3 9.1 multiply_reduce_fusion.2
  1569.2 4.4 fusion.54
  1573.6 4.3 fusion.53
  1578.4 15.1 convolution_bitcast_fusion.1
  1593.5 5.3 convolution_bitcast_fusion.4
  1598.8 9.8 convolution_bitcast_fusion.3
  1608.6 4.7 fusion.56
  1614.0 24.1 %all-reduce.1 = (f32[6,288]{1,0:T(8,128)}, f32[2,288]{1,0:T(2,128)}, f32[1152]{0:T(1024)}, f32[1152]{0:T(1024)}, f32[1152]{0:T(1024)}) all-reduce(f32[6,288]{1,0:T(8,128)S(1)} %convert_reduce_fusion.6, f32[2,288]{1,0:T(2,128)S(1)} %pad_maximum_fusion.3, f32[1152]{0:T(1024)S(1)} %copy-done.42, ...), channel_id=1, replica_groups=mesh['dp'=8,'tensor'=4] {'dp'}, use_global_device_ids=true, to_apply=%region_25.26 | all-reduce | flops 5760 | bytes 46080 | tf_op jit(solution)/shard_map/psum | solution.py:188
  1638.2 128.6 %all-reduce.14.cloned.1.call-done = (f32[1000,1152]{1,0:T(8,128)}, f32[1001,1152]{1,0:T(8,128)}) async-done(((f32[1000,1152]{1,0:T(8,128)}, f32[1001,1152]{1,0:T(8,128)}), (f32[1000,1152]{1,0:T(8,128)}, f32[1001,1152]{1,0:T(8,128)})) %all-reduce.14.cloned.1.call-update) | async-done | bytes 9220624 | tf_op jit(solution)/shard_map/psum | solution.py:205
  1766.7 300.5 %all-reduce.16.cloned.1.call-done = (f32[1152,6,288]{0,2,1:T(8,128)}, f32[1152,3,288]{0,2,1:T(8,128)}, f32[288,1152]{1,0:T(8,128)}, f32[1152,1152]{1,0:T(8,128)}, f32[1152,1152]{1,0:T(8,128)}) async-done(((f32[1152,6,288]{0,2,1:T(8,128)}, f32[1152,3,288]{0,2,1:T(8,128)}, f32[288,1152]{1,0:T(8,128)}, f32[1152,1152]{1,0:T(8,128)}, f32[1152,1152]{1,0:T(8,128)}), (f32[1152,6,288]{0,2,1:T(8,128)}, ...) | async-done | bytes 23887888 | tf_op jit(solution)/shard_map/psum | solution.py:188
  2067.2 5.1 copy.107
  2072.3 2.4 copy.108
  2075.1 1.6 slice-done.13
  2076.8 4.0 copy.109
  2081.8 1.9 copy.110
  2083.7 1.1 copy.111
  2084.8 2.7 copy.112
  2088.0 1.5 slice-done.15
  2089.6 2.4 copy.113
  (199 shorter events, 8.8 us)
Async XLA Ops:
  7.2 509.5 %copy-start = (bf16[1152,1152]{1,0:T(8,128)(2,1)S(1)}, bf16[1152,1152]{1,0:T(8,128)(2,1)}, u32[]{:S(2)}) copy-start(bf16[1152,1152]{1,0:T(8,128)(2,1)} %param.32) | copy-start | bytes 7962628
  7.2 7.8 copy-start.46
  7.2 7.9 copy-start.50
  7.2 8.3 copy-start.52
  7.2 483.1 %all-reduce.10.cloned.1.call-start = ((), (), s32[]{:S(2)}) async-start(), calls=%async_computation | async-start | bytes 18874368 | tf_op jit(solution)/shard_map/psum | solution.py:100
  7.3 7.8 copy-start.15
  7.3 8.3 copy-start.14
  7.3 9.4 copy-start.6
  10.5 128.8 %copy-start.32 = (f32[8,256]{1,0:T(8,128)}, f32[8,256]{1,0:T(8,128)S(1)}, u32[]{:S(2)}) copy-start(f32[8,256]{1,0:T(8,128)S(1)} %broadcast_multiply_fusion.5) | copy-start | bytes 24580
  15.0 124.3 %copy-start.34 = (f32[8,256]{1,0:T(8,128)}, f32[8,256]{1,0:T(8,128)S(1)}, u32[]{:S(2)}) copy-start(f32[8,256]{1,0:T(8,128)S(1)} %add_rsqrt_fusion.1) | copy-start | bytes 24580
  135.9 11.2 copy-start.38
  139.3 7.9 copy-start.28
  151.1 5.2 copy-start.44
  151.2 5.2 copy-start.9
  159.6 6.1 copy-start.47
  159.6 6.1 copy-start.48
  165.0 700.2 %all-reduce.12.cloned.1.call-start = ((), (), s32[]{:S(2)}) async-start(), calls=%async_computation.1 | async-start | bytes 18874368 | tf_op jit(solution)/shard_map/psum | solution.py:125
  165.7 324.6 %copy-start.36 = (f32[1152]{0:T(1024)}, f32[1152]{0:T(1024)S(1)}, u32[]{:S(2)}) copy-start(f32[1152]{0:T(1024)S(1)} %convert_element_type.142) | copy-start | bytes 13828
  180.0 336.7 %copy-start.54 = (f32[8]{0:T(128)}, f32[8]{0:T(128)S(1)}, u32[]{:S(2)}) copy-start(f32[8]{0:T(128)S(1)} %compare_convert_fusion) | copy-start | bytes 100
  490.3 15.3 copy-start.57
  500.7 6.4 copy-start.2
  500.7 6.4 copy-start.40
  500.7 15.9 slice-start.10
  507.1 9.6 slice-start.11
  541.5 995.5 %all-reduce.18.cloned.1.call-start = ((), (), s32[]{:S(2)}) async-start(), calls=%async_computation.4 | async-start | bytes 37748736 | tf_op jit(solution)/shard_map/psum | solution.py:110
  555.3 318.4 %copy-start.55 = (f32[8]{0:T(128)S(1)}, f32[8]{0:T(128)}, u32[]{:S(2)}) copy-start(f32[8]{0:T(128)} %copy-done.54) | copy-start | bytes 100
  865.2 9.2 copy-start.4
  885.8 5.2 slice-start.1
  887.6 5.2 copy-start.10
  887.6 5.2 copy-start.45
  892.8 7.6 copy-start.19
  900.4 8.0 copy-start.23
  908.4 858.3 %all-reduce.14.cloned.1.call-start = ((), (), s32[]{:S(2)}) async-start(), calls=%async_computation.2 | async-start | bytes 18505728 | tf_op jit(solution)/shard_map/psum | solution.py:205
  909.1 627.9 %copy-start.29 = (f32[8,1152]{1,0:T(8,128)S(1)}, f32[8,1152]{1,0:T(8,128)}, u32[]{:S(2)}) copy-start(f32[8,1152]{1,0:T(8,128)} %copy-done.28) | copy-start | bytes 110596
  909.1 627.9 %copy-start.33 = (f32[8,256]{1,0:T(8,128)S(1)}, f32[8,256]{1,0:T(8,128)}, u32[]{:S(2)}) copy-start(f32[8,256]{1,0:T(8,128)} %copy-done.32) | copy-start | bytes 24580
  909.1 627.9 %copy-start.35 = (f32[8,256]{1,0:T(8,128)S(1)}, f32[8,256]{1,0:T(8,128)}, u32[]{:S(2)}) copy-start(f32[8,256]{1,0:T(8,128)} %copy-done.34) | copy-start | bytes 24580
  1537.0 22.2 %slice-start.2 = ((s8[4718592]{0:T(1024)(128)(4,1)}), s8[4194304]{0:T(1024)(128)(4,1)S(1)}, s32[]{:S(2)}) async-start(s8[4718592]{0:T(1024)(128)(4,1)} %bitcast.124), calls=%async_computation.7 | async-start | bytes 8388608
  1537.0 22.2 %slice-start.4 = ((s8[9437184]{0:T(1024)(128)(4,1)}), s8[4194304]{0:T(1024)(128)(4,1)S(1)}, s32[]{:S(2)}) async-start(s8[9437184]{0:T(1024)(128)(4,1)} %bitcast.126), calls=%async_computation.9 | async-start | bytes 8388608
  1537.0 22.2 %slice-start.5 = ((s8[9437184]{0:T(1024)(128)(4,1)}), s8[4194304]{0:T(1024)(128)(4,1)S(1)}, s32[]{:S(2)}) async-start(s8[9437184]{0:T(1024)(128)(4,1)} %bitcast.126), calls=%async_computation.10 | async-start | bytes 8388608
  1537.0 22.2 %slice-start.7 = ((s8[9437184]{0:T(1024)(128)(4,1)}), s8[4194304]{0:T(1024)(128)(4,1)S(1)}, s32[]{:S(2)}) async-start(s8[9437184]{0:T(1024)(128)(4,1)} %bitcast.128), calls=%async_computation.12 | async-start | bytes 8388608
  1537.0 22.2 %slice-start.8 = ((s8[9437184]{0:T(1024)(128)(4,1)}), s8[4194304]{0:T(1024)(128)(4,1)S(1)}, s32[]{:S(2)}) async-start(s8[9437184]{0:T(1024)(128)(4,1)} %bitcast.128), calls=%async_computation.13 | async-start | bytes 8388608
  1545.9 13.3 slice-start.3
  1545.9 13.3 slice-start.6
  1545.9 13.3 slice-start.9
  1545.9 13.3 copy-start.37
  1559.3 9.2 copy-start.7
  1559.3 9.2 copy-start.27
  1559.3 9.9 copy-start.51
  1568.4 5.2 copy-start.53
  1569.2 9.2 copy-start.41
  1577.9 15.6 copy-start.18
  1577.9 489.3 %all-reduce.16.cloned.1.call-start = ((), (), s32[]{:S(2)}) async-start(), calls=%async_computation.3 | async-start | bytes 47775744 | tf_op jit(solution)/shard_map/psum | solution.py:188
  1593.5 5.3 copy-start.20
  1593.5 5.3 copy-start.22
  1593.5 5.3 copy-start.24
  1593.5 5.3 copy-start.39
  2067.2 5.1 copy-start.12
  2067.2 7.9 slice-start.12
  2072.3 12.5 slice-start.16
  2076.8 5.0 copy-start.13
  2076.8 7.0 copy-start.16
  2076.8 8.0 slice-start.17
  2083.7 8.2 copy-start.1
  2084.8 4.7 slice-start.15
  (19 other events, 42.5 us)
Sparse Core Ops, SparseCore 0:
  165.1 325.1 all-reduce.9
  541.6 323.5 all-reduce.11
  908.5 628.3 all-reduce.17
  1578.0 188.6 all-reduce.13
  1772.5 294.6 all-reduce.15
where the time goes:
time: 2100 us
  waiting for transfers between devices  1660 us (79%)
  matrix products  144 us (7%)
  blocking collectives  115 us (5%)
  local copies, waits for them, and re-layouts  84.7 us (4%)
  other arithmetic  78.3 us (4%)
    psum x1, waiting for transfers between devices, local(): branch = lax.psum(mlp_part, 'tensor') + down_bias.astype(wide)  611 us
    psum x1, waiting for transfers between devices, local(): attention = lax.psum(attn_part, 'tensor') + proj_bias.astype(wide)  310 us
    psum x1, waiting for transfers between devices, local(): d_hidden_mlp = lax.psum(d_mlp_part, 'tensor')  310 us
    psum x1, waiting for transfers between devices, local(): lax.psum((grad_qkv_weight, grad_qv_bias, grad_proj_weight, grad_proj_bias...  300 us
    psum x1, waiting for transfers between devices, local(): lax.psum((grad_time_table, grad_class_table), ('dp', 'tensor'))  129 us
    all_gather x1, blocking collectives, local(): modulation = lax.all_gather(mod_local, 'tensor', axis=2, tiled=True)  91.1 us
    unnamed x174, local copies, waits for them, and re-layouts  57 us
  transfers between devices with their start and end apart: 5, of which 5 were waited for; matrix products, arithmetic and copies ran while one was open for 4% of the time, Pallas kernels for 0%

commit v1 on v0

--- a/solution.py
+++ b/solution.py
@@ -7,6 +7,17 @@
 EPSILON = 1e-06
 GELU_ROOT = 0.7978845608028654
 GELU_CUBIC = 0.044715
+
+
+def detail_shards_on(vals):
+    nodes = lax.psum(1, "tensor")
+    moved = lambda arr_now: [(jj, jj ^ arr_now) for jj in range(nodes)]
+    work_now = vals
+    for tick in range(nodes.bit_length() - 1):
+        a_now = moved(1 << tick)
+        outer = lax.ppermute(work_now, "tensor", a_now)
+        work_now = work_now + outer
+    return work_now
 
 
 def norm_parts(values):
@@ -122,7 +133,7 @@
         (grad_down_weight, grad_down_bias, grad_up_weight, grad_up_bias), "dp"
     )
     d_mlp_part = jnp.einsum("gsf,df->gsd", d_pre, up_weight, preferred_element_type=wide)
-    d_hidden_mlp = lax.psum(d_mlp_part, "tensor")
+    d_hidden_mlp = detail_shards_on(d_mlp_part)
     d_shift_mlp = jnp.sum(d_hidden_mlp, axis=1)
     d_scale_mlp = jnp.sum(d_hidden_mlp * normed_mlp, axis=1)
     d_middle = grad_out + norm_back(d_hidden_mlp * (1.0 + scale_mlp), normed_mlp, inverse_mlp)

time: 2100 us -> 2390 us (1.14)
  waiting for transfers between devices: 1660 us -> 1950 us
    ppermute x0 -> x2, waiting for transfers between devices: none -> 593 us  [detail_shards_on(): outer = lax.ppermute(work_now, 'tensor', a_now)]
    psum x1 -> x0, waiting for transfers between devices: 310 us -> none  [local(): d_hidden_mlp = lax.psum(d_mlp_part, 'tensor')]
    unnamed x174 -> x178, local copies, waits for them, and re-layouts: 57 us -> 53.4 us
  transfers between devices with their start and end apart: 5 -> 6, of which waited for: 5 -> 6; matrix products, arithmetic and copies ran while one was open for 4% -> 3% of each run, Pallas kernels for 0% -> 0%
where the time goes in v1:
time: 2390 us
  waiting for transfers between devices  1950 us (82%)
  matrix products  144 us (6%)
  blocking collectives  115 us (5%)
  other arithmetic  86.7 us (4%)
  local copies, waits for them, and re-layouts  81.1 us (3%)
    psum x1, waiting for transfers between devices, local(): branch = lax.psum(mlp_part, 'tensor') + down_bias.astype(wide)  612 us
    ppermute x2, waiting for transfers between devices, detail_shards_on(): outer = lax.ppermute(work_now, 'tensor', a_now)  593 us
    psum x1, waiting for transfers between devices, local(): attention = lax.psum(attn_part, 'tensor') + proj_bias.astype(wide)  311 us
    psum x1, waiting for transfers between devices, local(): lax.psum((grad_qkv_weight, grad_qv_bias, grad_proj_weight, grad_proj_bias...  301 us
    psum x1, waiting for transfers between devices, local(): lax.psum((grad_time_table, grad_class_table), ('dp', 'tensor'))  129 us
    all_gather x1, blocking collectives, local(): modulation = lax.all_gather(mod_local, 'tensor', axis=2, tiled=True)  90.6 us
    unnamed x178, local copies, waits for them, and re-layouts  53.4 us
  transfers between devices with their start and end apart: 6, of which 6 were waited for; matrix products, arithmetic and copies ran while one was open for 3% of the time, Pallas kernels for 0%

profile of v1, /device:TPU:0, one launch (start us, length us, event | category | flops | bytes accessed | tf_op | source)
XLA Modules:
  0.0 2390.0 jit_solution(13938781230262972079)
XLA Ops:
  7.3 3.2 convert_reduce_fusion
  10.5 4.5 fusion.14
  16.6 1.3 convolution_add_fusion.1
  18.0 1.5 copy.58
  19.4 90.6 %all_gather.3 = f32[8,6,1152]{1,0,2:T(8,128)} all-gather(f32[8,6,288]{1,0,2:T(8,128)} %copy.58), channel_id=1, replica_groups=mesh['dp'=8,'tensor'=4] {'tensor'}, dimensions={2}, use_global_device_ids=true | all-gather | bytes 276480 | tf_op jit(solution)/shard_map/all_gather | solution.py:84
  110.1 22.1 fusion.73
  132.1 3.3 copy.86
  135.5 3.3 copy.85
  138.9 7.8 fusion.40
  146.7 1.1 slice.59
  147.9 2.7 fusion.72
  150.7 3.5 multiply_reduce_fusion.8
  154.3 1.6 fusion.22
  155.9 2.2 fusion.42
  158.1 1.0 copy-done.17
  159.1 5.5 fusion.49
  165.4 3.3 copy.87
  168.7 3.6 copy.88
  172.4 3.3 copy.84
  175.7 3.3 copy.89
  179.1 310.9 %all-reduce.9.cloned.1.call-done = f32[8,256,1152]{2,1,0:T(8,128)} async-done(((f32[8,256,1152]{2,1,0:T(8,128)}), f32[8,256,1152]{2,1,0:T(8,128)}) %all-reduce.9.cloned.1.call-update) | async-done | bytes 9437200 | tf_op jit(solution)/shard_map/psum | solution.py:111
  490.0 10.4 fusion.71
  500.4 4.9 multiply_reduce_fusion.4
  505.3 1.4 copy-done.2
  506.8 9.6 fusion.35
  516.4 13.2 convert_reduce_fusion.2
  529.6 7.1 fusion.33
  536.8 3.6 copy-done.9
  540.3 201.0 %collective-permute-done = f32[8,256,1152]{2,1,0:T(8,128)} collective-permute-done((f32[8,256,1152]{2,1,0:T(8,128)S(1)}, f32[8,256,1152]{2,1,0:T(8,128)}, u32[]{:S(2)}, u32[]{:S(2)}) %collective-permute-start) | collective-permute-done | bytes 9437216 | tf_op jit(solution)/shard_map/ppermute | solution.py:18
  741.3 11.0 add.213
  752.4 1.4 collective-permute-start.1
  753.8 13.3 fusion.31
  767.1 392.3 %collective-permute-done.1 = f32[8,256,1152]{2,1,0:T(8,128)} collective-permute-done((f32[8,256,1152]{2,1,0:T(8,128)}, f32[8,256,1152]{2,1,0:T(8,128)}, u32[]{:S(2)}, u32[]{:S(2)}) %collective-permute-start.1) | collective-permute-done | bytes 9437216 | tf_op jit(solution)/shard_map/ppermute | solution.py:18
  1159.5 9.2 multiply_reduce_fusion.1
  1168.7 8.1 convert_reduce_fusion.3
  1176.8 4.2 convolution_convert_fusion
  1181.7 1.8 convert_reduce_fusion.4
  1183.5 2.6 multiply_reduce_fusion.5
  1186.1 2.2 multiply_convert_fusion.4
  1188.4 1.4 multiply_convert_fusion.5
  1190.9 8.0 convolution_bitcast_fusion.2
  1199.5 16.2 convolution_bitcast_fusion
  1215.7 612.2 %all-reduce.15.cloned.1.call-done = (f32[8,256,1152]{2,1,0:T(8,128)}, f32[8,256,1152]{2,1,0:T(8,128)}) async-done(((f32[8,256,1152]{2,1,0:T(8,128)}, f32[8,256,1152]{2,1,0:T(8,128)}), (f32[8,256,1152]{2,1,0:T(8,128)}, f32[8,256,1152]{2,1,0:T(8,128)})) %all-reduce.15.cloned.1.call-update) | async-done | bytes 18874384 | tf_op jit(solution)/shard_map/psum | solution.py:121
  1828.0 9.1 fusion.13
  1837.2 13.2 convert_reduce_fusion.1
  1850.6 9.1 multiply_reduce_fusion.2
  1860.5 4.4 fusion.54
  1864.9 4.3 fusion.53
  1869.4 15.0 convolution_bitcast_fusion.1
  1884.5 5.3 convolution_bitcast_fusion.4
  1889.8 9.9 convolution_bitcast_fusion.3
  1899.7 4.7 fusion.56
  1905.1 24.3 %all-reduce.1 = (f32[6,288]{1,0:T(8,128)}, f32[2,288]{1,0:T(2,128)}, f32[1152]{0:T(1024)}, f32[1152]{0:T(1024)}, f32[1152]{0:T(1024)}) all-reduce(f32[6,288]{1,0:T(8,128)S(1)} %convert_reduce_fusion.6, f32[2,288]{1,0:T(2,128)S(1)} %pad_maximum_fusion.3, f32[1152]{0:T(1024)S(1)} %copy-done.41, ...), channel_id=1, replica_groups=mesh['dp'=8,'tensor'=4] {'dp'}, use_global_device_ids=true, to_apply=%region_24.25 | all-reduce | flops 5760 | bytes 46080 | tf_op jit(solution)/shard_map/psum | solution.py:199
  1929.3 128.7 %all-reduce.11.cloned.1.call-done = (f32[1000,1152]{1,0:T(8,128)}, f32[1001,1152]{1,0:T(8,128)}) async-done(((f32[1000,1152]{1,0:T(8,128)}, f32[1001,1152]{1,0:T(8,128)}), (f32[1000,1152]{1,0:T(8,128)}, f32[1001,1152]{1,0:T(8,128)})) %all-reduce.11.cloned.1.call-update) | async-done | bytes 9220624 | tf_op jit(solution)/shard_map/psum | solution.py:216
  2058.0 300.5 %all-reduce.13.cloned.1.call-done = (f32[1152,6,288]{0,2,1:T(8,128)}, f32[1152,3,288]{0,2,1:T(8,128)}, f32[288,1152]{1,0:T(8,128)}, f32[1152,1152]{1,0:T(8,128)}, f32[1152,1152]{1,0:T(8,128)}) async-done(((f32[1152,6,288]{0,2,1:T(8,128)}, f32[1152,3,288]{0,2,1:T(8,128)}, f32[288,1152]{1,0:T(8,128)}, f32[1152,1152]{1,0:T(8,128)}, f32[1152,1152]{1,0:T(8,128)}), (f32[1152,6,288]{0,2,1:T(8,128)}, ...) | async-done | bytes 23887888 | tf_op jit(solution)/shard_map/psum | solution.py:199
  2358.5 5.1 copy.106
  2363.6 2.4 copy.107
  2366.4 1.6 slice-done.18
  2368.0 4.0 copy.108
  2373.1 1.9 copy.109
  2375.0 1.1 copy.110
  2376.1 2.7 copy.111
  2379.3 1.5 slice-done.20
  2380.8 2.4 copy.112
  (207 shorter events, 8.2 us)
Async XLA Ops:
  7.2 509.2 %copy-start = (bf16[1152,1152]{1,0:T(8,128)(2,1)S(1)}, bf16[1152,1152]{1,0:T(8,128)(2,1)}, u32[]{:S(2)}) copy-start(bf16[1152,1152]{1,0:T(8,128)(2,1)} %param.32) | copy-start | bytes 7962628
  7.2 7.8 copy-start.45
  7.2 7.9 copy-start.49
  7.2 8.3 copy-start.51
  7.2 482.7 %all-reduce.9.cloned.1.call-start = ((), (), s32[]{:S(2)}) async-start(), calls=%async_computation | async-start | bytes 18874368 | tf_op jit(solution)/shard_map/psum | solution.py:111
  7.3 7.8 copy-start.15
  7.3 8.3 copy-start.14
  7.3 9.4 copy-start.6
  10.5 128.3 %copy-start.31 = (f32[8,256]{1,0:T(8,128)}, f32[8,256]{1,0:T(8,128)S(1)}, u32[]{:S(2)}) copy-start(f32[8,256]{1,0:T(8,128)S(1)} %broadcast_multiply_fusion.5) | copy-start | bytes 24580
  15.0 123.8 %copy-start.33 = (f32[8,256]{1,0:T(8,128)}, f32[8,256]{1,0:T(8,128)S(1)}, u32[]{:S(2)}) copy-start(f32[8,256]{1,0:T(8,128)S(1)} %add_rsqrt_fusion.1) | copy-start | bytes 24580
  135.5 11.2 copy-start.37
  138.8 7.9 copy-start.29
  150.7 5.2 copy-start.42
  150.7 5.2 copy-start.10
  159.1 6.2 copy-start.46
  159.1 6.2 copy-start.47
  164.6 1663.3 %all-reduce.15.cloned.1.call-start = ((), (), s32[]{:S(2)}) async-start(), calls=%async_computation.3 | async-start | bytes 37748736 | tf_op jit(solution)/shard_map/psum | solution.py:121
  165.4 324.6 %copy-start.35 = (f32[1152]{0:T(1024)}, f32[1152]{0:T(1024)S(1)}, u32[]{:S(2)}) copy-start(f32[1152]{0:T(1024)S(1)} %convert_element_type.142) | copy-start | bytes 13828
  179.0 326.3 %copy-start.39 = (f32[8,1,1152]{2,0,1:T(8,128)}, f32[8,1,1152]{2,0,1:T(8,128)S(1)}, u32[]{:S(2)}) copy-start(f32[8,1,1152]{2,0,1:T(8,128)S(1)} %copy.89) | copy-start | bytes 110596
  490.0 15.4 copy-start.54
  500.4 6.4 copy-start.2
  500.4 15.9 slice-start.13
  506.8 9.6 slice-start.14
  529.6 7.1 copy-start.56
  536.7 204.7 %collective-permute-start = (f32[8,256,1152]{2,1,0:T(8,128)S(1)}, f32[8,256,1152]{2,1,0:T(8,128)}, u32[]{:S(2)}, u32[]{:S(2)}) collective-permute-start(f32[8,256,1152]{2,1,0:T(8,128)S(1)} %fusion.33), channel_id=1, source_target_pairs={{0,1},{1,0},{2,3},{3,2},{4,5},{5,4},{6,7},{7,6},{8,9},{9,8},{10,11... | collective-permute-start | bytes 28311560 | tf_op jit(solution)/shard_map/ppermute | solution.py:18
  741.3 427.3 %slice-start.15 = ((s8[4718592]{0:T(1024)(128)(4,1)}), s8[524288]{0:T(1024)(128)(4,1)S(1)}, s32[]{:S(2)}) async-start(s8[4718592]{0:T(1024)(128)(4,1)} %bitcast.136), calls=%async_computation.19 | async-start | bytes 1048576
  752.4 407.1 %collective-permute-start.1 = (f32[8,256,1152]{2,1,0:T(8,128)}, f32[8,256,1152]{2,1,0:T(8,128)}, u32[]{:S(2)}, u32[]{:S(2)}) collective-permute-start(f32[8,256,1152]{2,1,0:T(8,128)} %add.213), channel_id=1, source_target_pairs={{0,2},{1,3},{2,0},{3,1},{4,6},{5,7},{6,4},{7,5},{8,10},{9,11},{10,... | collective-permute-start | bytes 28311560 | tf_op jit(solution)/shard_map/ppermute | solution.py:18
  753.8 405.7 %copy-start.4 = (f32[8,256,1152]{2,1,0:T(8,128)S(1)}, f32[8,256,1152]{2,1,0:T(8,128)}, u32[]{:S(2)}) copy-start(f32[8,256,1152]{2,1,0:T(8,128)} %add.213) | copy-start | bytes 28311556
  753.8 414.9 %slice-start = ((s8[9437184]{0:T(1024)(128)(4,1)}), s8[4194304]{0:T(1024)(128)(4,1)S(1)}, s32[]{:S(2)}) async-start(s8[9437184]{0:T(1024)(128)(4,1)} %bitcast.122), calls=%async_computation.4 | async-start | bytes 8388608
  753.8 414.9 %slice-start.1 = ((s8[9437184]{0:T(1024)(128)(4,1)}), s8[1048576]{0:T(1024)(128)(4,1)S(1)}, s32[]{:S(2)}) async-start(s8[9437184]{0:T(1024)(128)(4,1)} %bitcast.122), calls=%async_computation.5 | async-start | bytes 2097152
  753.8 414.9 %slice-start.16 = ((s8[4718592]{0:T(1024)(128)(4,1)}), s8[4194304]{0:T(1024)(128)(4,1)S(1)}, s32[]{:S(2)}) async-start(s8[4718592]{0:T(1024)(128)(4,1)} %bitcast.136), calls=%async_computation.20 | async-start | bytes 8388608
  767.1 401.6 %slice-start.2 = ((s8[9437184]{0:T(1024)(128)(4,1)}), s8[4194304]{0:T(1024)(128)(4,1)S(1)}, s32[]{:S(2)}) async-start(s8[9437184]{0:T(1024)(128)(4,1)} %bitcast.122), calls=%async_computation.6 | async-start | bytes 8388608
  1168.7 8.1 copy-start.26
  1183.5 7.4 copy-start.19
  1190.8 8.0 copy-start.23
  1198.8 859.1 %all-reduce.11.cloned.1.call-start = ((), (), s32[]{:S(2)}) async-start(), calls=%async_computation.1 | async-start | bytes 18505728 | tf_op jit(solution)/shard_map/psum | solution.py:216
  1199.5 628.4 %copy-start.30 = (f32[8,1152]{1,0:T(8,128)S(1)}, f32[8,1152]{1,0:T(8,128)}, u32[]{:S(2)}) copy-start(f32[8,1152]{1,0:T(8,128)} %copy-done.29) | copy-start | bytes 110596
  1199.5 628.4 %copy-start.32 = (f32[8,256]{1,0:T(8,128)S(1)}, f32[8,256]{1,0:T(8,128)}, u32[]{:S(2)}) copy-start(f32[8,256]{1,0:T(8,128)} %copy-done.31) | copy-start | bytes 24580
  1199.5 628.4 %copy-start.34 = (f32[8,256]{1,0:T(8,128)S(1)}, f32[8,256]{1,0:T(8,128)}, u32[]{:S(2)}) copy-start(f32[8,256]{1,0:T(8,128)} %copy-done.33) | copy-start | bytes 24580
  1828.0 22.5 slice-start.5
  1828.0 22.5 slice-start.7
  1828.0 22.5 slice-start.8
  1828.0 22.5 slice-start.10
  1828.0 22.5 slice-start.11
  1837.1 13.3 slice-start.6
  1837.2 13.3 slice-start.9
  1837.2 13.3 slice-start.12
  1837.2 13.3 copy-start.36
  1850.5 9.2 copy-start.7
  1850.5 9.2 copy-start.28
  1850.6 9.9 copy-start.50
  1859.7 5.2 copy-start.52
  1860.5 9.0 copy-start.40
  1869.2 15.3 copy-start.18
  1869.2 489.3 %all-reduce.13.cloned.1.call-start = ((), (), s32[]{:S(2)}) async-start(), calls=%async_computation.2 | async-start | bytes 47775744 | tf_op jit(solution)/shard_map/psum | solution.py:199
  1884.5 5.3 copy-start.20
  1884.5 5.3 copy-start.22
  1884.5 5.3 copy-start.24
  1884.5 5.3 copy-start.38
  2358.5 7.9 slice-start.17
  2363.6 12.5 slice-start.21
  2368.0 7.0 copy-start.16
  2368.0 8.0 slice-start.22
  2375.0 8.2 copy-start.1
  (22 other events, 63.0 us)
Sparse Core Ops, SparseCore 0:
  164.8 325.1 all-reduce.8
  1199.0 628.9 all-reduce.14
  1869.3 188.6 all-reduce.10
  2063.7 294.7 all-reduce.12
